TPU v7x, 32 devices: a whole 2x2x4 slice. The times are simulated.
32 devices in a mesh: group: 4 (over x, core), head: 8 (over z, y).
Axes of the slice: x: 2, y: 2, z: 4, core: 2. Of those that a mesh axis runs over, the one named last changes fastest.
Arguments:
- qkv: bfloat16 [2048, 3, 512], P(('group', 'head')), may hold values from -40 to 40
- pattern: int32 [4, 3, 8, 6], P('group'), may hold values from 0 to 7, as said below
- counts: int32 [4, 3, 8], P('group'), may hold values from 0 to 6, as said below
Outputs:
- attended: bfloat16 [2048, 512], P(('group', 'head'))
Inputs may be any that keep to these rules, and one draw needn't show every extreme that they name: `pattern`: within one list (g, j, n) the 6 blocks are distinct; at offset index 1 the first entry of query block n's list is n. `counts`: at offset index 1 every count is 1 or more; some count equals 6.
All inputs are finite; a program needn't handle non-finite values.
Results may differ from a plain program's by a relative error of at most 0.0044.
Values may be sent and summed in bfloat16 or wider, within the bound.
No kernel may reach another device: no remote copies, remote signals or barrier semaphores. Data moves between devices by JAX's collectives and lax.ppermute only.
A program may use at most 64 MiB of HBM per device.

v0:
```python
import jax
import jax.numpy as jnp
from jax import lax
from jax.sharding import PartitionSpec as P

BLOCK = 64


def from_behind(value, axis, steps):
    count = lax.axis_size(axis)
    pairs = [(source, (source + steps) % count) for source in range(count)]
    return lax.ppermute(value, axis, pairs)


def body(qkv, pattern, counts):
    half = lax.axis_size("group") // 4
    gathered = lax.all_to_all(qkv, "head", split_axis=2, concat_axis=0, tiled=True)
    group_rows = gathered.shape[0]
    head_dim = gathered.shape[2]
    blocks = group_rows // BLOCK
    query = gathered[:, 0].reshape(blocks, BLOCK, head_dim)
    paired = jnp.concatenate([gathered[:, 1], gathered[:, 2]], axis=-1)
    lists = pattern[0]
    live_counts = counts[0]
    scale = head_dim ** (-0.5)

    def attend(state, source, offset, keep):
        chosen = lax.dynamic_index_in_dim(lists, offset, 0, keepdims=False)
        number = lax.dynamic_index_in_dim(live_counts, offset, 0, keepdims=False) * keep
        width = chosen.shape[1]
        tiles = source.reshape(blocks, BLOCK, 2 * head_dim)[chosen]
        tiles = tiles.reshape(blocks, width * BLOCK, 2 * head_dim)
        key_part = tiles[..., :head_dim]
        value_part = tiles[..., head_dim:]
        scores = (
            jnp.einsum("nqd,nkd->nqk", query, key_part, preferred_element_type=jnp.float32) * scale
        )
        live = (jnp.arange(width * BLOCK, dtype=jnp.int32) // BLOCK)[None, :] < number[:, None]
        scores = jnp.where(live[:, None, :], scores, -jnp.inf)
        running, total, accum = state
        newmax = jnp.maximum(running, scores.max(axis=-1))
        weights = jnp.exp(scores - newmax[..., None])
        factor = jnp.exp(running - newmax)
        total = total * factor + weights.sum(axis=-1)
        accum = accum * factor[..., None] + jnp.einsum(
            "nqk,nkd->nqd",
            weights.astype(jnp.bfloat16),
            value_part,
            preferred_element_type=jnp.float32,
        )
        return (newmax, total, accum)

    start = (
        jnp.full((blocks, BLOCK), -jnp.inf, jnp.float32),
        jnp.zeros((blocks, BLOCK), jnp.float32),
        jnp.zeros((blocks, BLOCK, head_dim), jnp.float32),
    )
    state = attend(start, paired, half, jnp.int32(1))

    def both_step(step_index, carry):
        ahead, behind, state = carry
        ahead = from_behind(ahead, "group", 1)
        behind = from_behind(behind, "group", -1)
        state = attend(state, ahead, half - step_index, jnp.int32(1))
        state = attend(state, behind, half + step_index, jnp.int32(1))
        return (ahead, behind, state)

    ahead, behind, state = lax.fori_loop(1, half + 1, both_step, (paired, paired, state))
    running, total, accum = state
    output = (accum / total[..., None]).astype(jnp.bfloat16).reshape(group_rows, head_dim)
    return lax.all_to_all(output, "head", split_axis=0, concat_axis=1, tiled=True)


def solution(mesh):
    return jax.shard_map(
        body,
        mesh=mesh,
        in_specs=(
            P(("group", "head"), None, None),
            P("group", None, None, None),
            P("group", None, None),
        ),
        out_specs=P(("group", "head"), None),
        check_vma=False,
    )
```

profile of v0, /device:TPU:0, one launch (start us, length us, event | category | flops | bytes accessed | tf_op | source)
XLA Modules:
  0.0 40.3 jit_solution(15031859175372729375)
XLA Ops:
  0.0 1.2 %copy.19 = bf16[64,3,512]{0,1,2:T(4,128)(2,1)S(1)} copy(bf16[64,3,512]{2,0,1:T(8,128)(2,1)} %param.3) | data formatting | bytes 393216 | tf_op args[0]
  1.2 1.0 %reshape.303 = bf16[8,2,6144]{2,1,0:T(2,128)(2,1)} reshape(bf16[512,3,64]{2,1,0:T(4,128)(2,1)S(1)} %bitcast.55) | data formatting | bytes 393216
  2.3 0.0 copy-start.1
  2.3 0.0 copy-start
  2.3 7.4 %all-to-all-start = ((bf16[8,2,6144]{2,1,0:T(2,128)(2,1)}), bf16[8,2,6144]{2,1,0:T(2,128)(2,1)S(1)}, u32[]{:S(2)}, u32[]{:S(2)}) async-start(bf16[8,2,6144]{2,1,0:T(2,128)(2,1)} %reshape.303), calls=%async_computation | async-start | bytes 393216 | tf_op jit(solution)/shard_map/all_to_all | solution.py:17
  9.7 0.0 copy-done.1
  9.7 0.0 copy-done
  9.8 0.1 copy.24
  9.8 0.1 reshape.283
  9.9 0.1 copy.21
  10.0 0.1 reshape.275
  10.1 0.1 copy.27
  10.2 0.1 reshape.291
  10.3 0.1 broadcast_compare_fusion.1
  10.4 7.3 %all-to-all-done = bf16[8,2,6144]{2,1,0:T(2,128)(2,1)S(1)} async-done(((bf16[8,2,6144]{2,1,0:T(2,128)(2,1)}), bf16[8,2,6144]{2,1,0:T(2,128)(2,1)S(1)}, u32[]{:S(2)}, u32[]{:S(2)}) %all-to-all-start) | async-done | bytes 196640 | tf_op jit(solution)/shard_map/all_to_all | solution.py:17
  17.7 0.3 reshape.304
  18.0 0.3 copy.20
  18.3 0.1 slice_bitcast_fusion.4
  18.4 0.1 pad_maximum_fusion.1
  18.5 0.1 collective-permute-start.1
  18.6 0.5 %collective-permute-start = (bf16[512,128]{1,0:T(8,128)(2,1)S(1)}, bf16[512,128]{1,0:T(8,128)(2,1)S(1)}, u32[]{:S(2)}, u32[]{:S(2)}) collective-permute-start(bf16[512,128]{1,0:T(8,128)(2,1)S(1)} %pad_maximum_fusion.1), channel_id=1, source_target_pairs={{0,8},{8,16},{16,24},{24,0},{1,9},{9,17},{17,25},{25,1},{2,10},{10... | collective-permute-start | bytes 393224 | tf_op jit(solution)/shard_map/while/body/eval_jaxpr/ppermute | solution.py:12
  19.1 0.1 pad_maximum_fusion
  19.2 0.7 %gather_fusion = bf16[48,64,128]{2,1,0:T(8,128)(2,1)S(1)} fusion(bf16[8,64,128]{2,1,0:T(8,128)(2,1)S(1)} %pad_maximum_fusion, s32[1024]{0:T(1024)S(1)} %pad_clamp_fusion.2), kind=kCustom, calls=%fused_computation | custom fusion | bytes 1573056 | tf_op jit(solution)/shard_map/gather | solution.py:31
  19.9 0.5 %fusion.32 = (f32[8,64]{1,0:T(8,128)S(1)}, f32[8,64,384]{2,1,0:T(8,128)S(1)}) fusion(bf16[8,64,64]{2,1,0:T(8,128)(2,1)S(1)} %bitcast.56, bf16[8,384,128]{2,1,0:T(8,128)(2,1)S(1)} %bitcast.46, pred[8,384]{1,0:T(8,128)(4,1)S(1)} %get-tuple-element.51), kind=kOutput, calls=%fused_computation.65 | convolution fusion | flops 25755136 | bytes 1643520 | tf_op jit(solution)/shard_map/nqd,nkd->nqk/dot_general | solution.py:36
  20.4 0.3 fusion.16
  20.8 3.7 %collective-permute-done = bf16[512,128]{1,0:T(8,128)(2,1)S(1)} collective-permute-done((bf16[512,128]{1,0:T(8,128)(2,1)S(1)}, bf16[512,128]{1,0:T(8,128)(2,1)S(1)}, u32[]{:S(2)}, u32[]{:S(2)}) %collective-permute-start) | collective-permute-done | bytes 131104 | tf_op jit(solution)/shard_map/while/body/eval_jaxpr/ppermute | solution.py:12
  24.4 0.7 %gather_fusion.1 = bf16[48,64,128]{2,1,0:T(8,128)(2,1)S(1)} fusion(bf16[8,64,128]{2,1,0:T(8,128)(2,1)S(1)} %bitcast.51, s32[1024]{0:T(1024)S(1)} %pad_clamp_fusion.1), kind=kCustom, calls=%fused_computation.1 | custom fusion | bytes 1573056 | tf_op jit(solution)/shard_map/while/body/eval_jaxpr/gather | solution.py:31
  25.1 0.0 collective-permute-done.1
  25.1 0.7 %gather_fusion.2 = bf16[48,64,128]{2,1,0:T(8,128)(2,1)S(1)} fusion(bf16[8,64,128]{2,1,0:T(8,128)(2,1)S(1)} %bitcast.50, s32[1024]{0:T(1024)S(1)} %pad_clamp_fusion), kind=kCustom, calls=%fused_computation.2 | custom fusion | bytes 1573056 | tf_op jit(solution)/shard_map/while/body/eval_jaxpr/gather | solution.py:31
  25.8 0.5 %fusion.33 = (f32[8,64]{1,0:T(8,128)S(1)}, f32[8,64,384]{2,1,0:T(8,128)S(1)}) fusion(bf16[8,64,64]{2,1,0:T(8,128)(2,1)S(1)} %bitcast.57, bf16[8,384,128]{2,1,0:T(8,128)(2,1)S(1)} %bitcast.52, pred[8,384]{1,0:T(8,128)(4,1)S(1)} %get-tuple-element.50), kind=kOutput, calls=%fused_computation.66 | convolution fusion | flops 25755136 | bytes 1643520 | tf_op jit(solution)/shard_map/while/body/eval_jaxpr/nqd,nkd->nqk/dot_general | solution.py:36
  26.4 0.5 %fusion.34 = (f32[8,64]{1,0:T(8,128)S(1)}, f32[8,64,384]{2,1,0:T(8,128)S(1)}) fusion(bf16[8,64,64]{2,1,0:T(8,128)(2,1)S(1)} %bitcast.58, bf16[8,384,128]{2,1,0:T(8,128)(2,1)S(1)} %bitcast.48, pred[8,384]{1,0:T(8,128)(4,1)S(1)} %get-tuple-element.49), kind=kOutput, calls=%fused_computation.67 | convolution fusion | flops 25755136 | bytes 1643520 | tf_op jit(solution)/shard_map/while/body/eval_jaxpr/nqd,nkd->nqk/dot_general | solution.py:36
  26.9 0.5 %fusion.18 = (f32[8,64]{1,0:T(8,128)S(1)}, f32[8,64]{1,0:T(8,128)S(1)}) fusion(f32[8,64,384]{2,1,0:T(8,128)S(1)} %get-tuple-element.60, f32[8,64]{1,0:T(8,128)S(1)} %get-tuple-element.27, f32[8,64,384]{2,1,0:T(8,128)S(1)} %get-tuple-element.58, f32[8,64]{1,0:T(8,128)S(1)} %get-tuple-element.26), kind=kLoop, calls=%fused_computation.30 | loop fusion | flops 785408 | bytes 1581056 | tf_op jit(solution)/shard_map/while/body/eval_jaxpr/reduce_sum | solution.py:44
  27.5 0.6 %fusion.8 = f32[8,64,64]{2,1,0:T(8,128)S(1)} fusion(bf16[8,384,128]{2,1,0:T(8,128)(2,1)S(1)} %bitcast.47, f32[8,64,384]{2,1,0:T(8,128)S(1)} %get-tuple-element.56, f32[8,64]{1,0:T(8,128)S(1)} %get-tuple-element.55, f32[8,64]{1,0:T(8,128)S(1)} %get-tuple-element.25, f32[8,64]{1,0:T(8,128)S(1)} %get-tuple-element.48), kind=kOutput, calls=%fused_computation.17 | convolution fusion | flops 25624576 | bytes 1710080 | tf_op jit(solution)/shard_map/nqk,nkd->nqd/dot_general | solution.py:45
  28.1 0.6 %fusion.7 = f32[8,64,64]{2,1,0:T(8,128)S(1)} fusion(f32[8,64,64]{2,1,0:T(8,128)S(1)} %fusion.8, bf16[8,384,128]{2,1,0:T(8,128)(2,1)S(1)} %bitcast.49, f32[8,64,384]{2,1,0:T(8,128)S(1)} %get-tuple-element.60, f32[8,64]{1,0:T(8,128)S(1)} %get-tuple-element.27, f32[8,64]{1,0:T(8,128)S(1)} %get-tuple-element.24), kind=kOutput, calls=%fused_computation.15 | convolution fusion | flops 25624576 | bytes 1839104 | tf_op jit(solution)/shard_map/while/body/eval_jaxpr/nqk,nkd->nqd/dot_general | solution.py:45
  28.7 0.6 %fusion.9 = bf16[8,64,64]{2,1,0:T(8,128)(2,1)S(1)} fusion(f32[8,64,64]{2,1,0:T(8,128)S(1)} %fusion.7, bf16[8,384,128]{2,1,0:T(8,128)(2,1)S(1)} %bitcast.53, f32[8,64,384]{2,1,0:T(8,128)S(1)} %get-tuple-element.58, f32[8,64]{1,0:T(8,128)S(1)} %get-tuple-element.26, f32[8,64]{1,0:T(8,128)S(1)} %get-tuple-element.23), kind=kOutput, calls=%fused_computation.18 | convolution fusion | flops 25657344 | bytes 1773568 | tf_op jit(solution)/shard_map/while/body/eval_jaxpr/nqk,nkd->nqd/dot_general | solution.py:45
  29.2 0.2 reshape.305
  29.4 9.8 %all_to_all.34 = bf16[8,2,2048]{2,1,0:T(2,128)(2,1)S(1)} all-to-all(bf16[8,2,2048]{2,1,0:T(2,128)(2,1)S(1)} %reshape.305), channel_id=1, replica_groups=mesh['group'=4,'head'=8] {'head'}, dimensions={0} | all-to-all | bytes 131072 | tf_op jit(solution)/shard_map/all_to_all | solution.py:71
  39.2 0.1 reshape.306
  39.4 0.1 copy.30
  39.5 0.8 %all_to_all.31 = bf16[64,512]{1,0:T(8,128)(2,1)} reshape(bf16[64,8,64]{2,1,0:T(8,128)(2,1)S(1)} %copy.30) | data formatting | bytes 131072 | tf_op jit(solution)/shard_map/all_to_all | solution.py:71
  (8 shorter events, 0.1 us)
Async XLA Ops:
  2.3 7.4 %copy-start.1 = (s32[1,3,8]{2,0,1:T(1,128)S(1)}, s32[1,3,8]{2,0,1:T(1,128)}, u32[]{:S(2)}) copy-start(s32[1,3,8]{2,0,1:T(1,128)} %param.5) | copy-start | bytes 292
  2.3 7.5 %copy-start = (s32[1,3,8,6]{2,0,3,1:T(1,128)S(1)}, s32[1,3,8,6]{2,0,3,1:T(1,128)}, u32[]{:S(2)}) copy-start(s32[1,3,8,6]{2,0,3,1:T(1,128)} %param.4) | copy-start | bytes 1732
  2.3 15.4 %all-to-all-start = ((bf16[8,2,6144]{2,1,0:T(2,128)(2,1)}), bf16[8,2,6144]{2,1,0:T(2,128)(2,1)S(1)}, u32[]{:S(2)}, u32[]{:S(2)}) async-start(bf16[8,2,6144]{2,1,0:T(2,128)(2,1)} %reshape.303), calls=%async_computation | async-start | bytes 393216 | tf_op jit(solution)/shard_map/all_to_all | solution.py:17
  18.5 6.6 %collective-permute-start.1 = (bf16[512,128]{1,0:T(8,128)(2,1)S(1)}, bf16[512,128]{1,0:T(8,128)(2,1)S(1)}, u32[]{:S(2)}, u32[]{:S(2)}) collective-permute-start(bf16[512,128]{1,0:T(8,128)(2,1)S(1)} %pad_maximum_fusion.1), channel_id=1, source_target_pairs={{0,24},{8,0},{16,8},{24,16},{1,25},{9,1},{17,9},{25,17},{2,26},{10... | collective-permute-start | bytes 393224 | tf_op jit(solution)/shard_map/while/body/eval_jaxpr/ppermute | solution.py:12
  18.6 5.8 %collective-permute-start = (bf16[512,128]{1,0:T(8,128)(2,1)S(1)}, bf16[512,128]{1,0:T(8,128)(2,1)S(1)}, u32[]{:S(2)}, u32[]{:S(2)}) collective-permute-start(bf16[512,128]{1,0:T(8,128)(2,1)S(1)} %pad_maximum_fusion.1), channel_id=1, source_target_pairs={{0,8},{8,16},{16,24},{24,0},{1,9},{9,17},{17,25},{25,1},{2,10},{10... | collective-permute-start | bytes 393224 | tf_op jit(solution)/shard_map/while/body/eval_jaxpr/ppermute | solution.py:12
where the time goes:
time: 40.6 us; the launch traced here: 40.3 us
  waiting for transfers between devices  11 us (27%)
  blocking collectives  9.85 us (24%)
  starting transfers between devices  7.99 us (20%)
  local copies, waits for them, and re-layouts  6.72 us (17%)
  matrix products  3.38 us (8%)
  other arithmetic  1.19 us (3%)
    all_to_all x1, blocking collectives, body(): lax.all_to_all(output, 'head', split_axis=0, concat_axis=1, tiled=True)  9.85 us
    all_to_all x1, starting transfers between devices, body(): lax.all_to_all(qkv, 'head', split_axis=2, concat_axis=0, tiled=True)  7.44 us
    all_to_all x1, waiting for transfers between devices, body(): lax.all_to_all(qkv, 'head', split_axis=2, concat_axis=0, tiled=True)  7.3 us
    ppermute x2, waiting for transfers between devices, from_behind(): return lax.ppermute(value, axis, pairs)  3.65 us
    unnamed x9, local copies, waits for them, and re-layouts  2.87 us
    gather x3, local copies, waits for them, and re-layouts, attend(): tiles = source.reshape(blocks, BLOCK, 2 * head_dim)[chosen]  2.09 us
    dot_general x3, matrix products, attend(): jnp.einsum('nqk,nkd->nqd', weights.astype(jnp.bfloat16), value_part, pref...  1.75 us
    dot_general x3, matrix products, attend(): jnp.einsum('nqd,nkd->nqk', query, key_part, preferred_element_type=jnp.fl...  1.63 us
  transfers between devices with their start and end apart: 3, of which 2 were waited for; matrix products, arithmetic and copies ran while one was open for 7% of the time, Pallas kernels for 0%

commit v1 on v0

--- a/solution.py
+++ b/solution.py
@@ -4,6 +4,17 @@
 from jax.sharding import PartitionSpec as P
 
 BLOCK = 64
+
+
+def split_up(value, dim, size):
+    before, after = (value.shape[:dim], value.shape[dim + 1 :])
+    return jnp.moveaxis(value.reshape(*before, size, -1, *after), dim, 0)
+
+
+def joined_along(pieces, dim):
+    pieces = jnp.moveaxis(pieces, 0, dim)
+    shape = pieces.shape
+    return pieces.reshape(*shape[:dim], shape[dim] * shape[dim + 1], *shape[dim + 2 :])
 
 
 def from_behind(value, axis, steps):
@@ -14,7 +25,14 @@
 
 def body(qkv, pattern, counts):
     half = lax.axis_size("group") // 4
-    gathered = lax.all_to_all(qkv, "head", split_axis=2, concat_axis=0, tiled=True)
+    devices, place = (lax.axis_size("head"), lax.axis_index("head"))
+    blocks_2 = split_up(qkv, 2, devices)
+    gathered_2 = [blocks_2[place]]
+    for step in range(1, devices):
+        sent = blocks_2[place ^ step]
+        gathered_2.append(lax.ppermute(sent, "head", [(i, i ^ step) for i in range(devices)]))
+    blocks_2 = jnp.stack(gathered_2)[place ^ jnp.arange(devices)]
+    gathered = joined_along(blocks_2, 0)
     group_rows = gathered.shape[0]
     head_dim = gathered.shape[2]
     blocks = group_rows // BLOCK

time: 40.6 us -> 45.5 us (1.12)
  starting transfers between devices: 7.99 us -> 13.9 us
  waiting for transfers between devices: 11 us -> 9.51 us
  local copies, waits for them, and re-layouts: 6.72 us -> 7.76 us
  blocking collectives: 9.85 us -> 9.29 us
    ppermute x0 -> x7, starting transfers between devices: none -> 13.3 us  [body(): lax.ppermute(sent, 'head', [(i, i ^ step) for i in range(devices)])]
    all_to_all x1 -> x0, starting transfers between devices: 7.44 us -> none  [body(): lax.all_to_all(qkv, 'head', split_axis=2, concat_axis=0, tiled=True)]
    all_to_all x1 -> x0, waiting for transfers between devices: 7.3 us -> none  [body(): lax.all_to_all(qkv, 'head', split_axis=2, concat_axis=0, tiled=True)]
    ppermute x0 -> x7, waiting for transfers between devices: none -> 6.25 us  [body(): lax.ppermute(sent, 'head', [(i, i ^ step) for i in range(devices)])]
    unnamed x9 -> x20, local copies, waits for them, and re-layouts: 2.87 us -> 0.45 us
    reshape x0 -> x2, local copies, waits for them, and re-layouts: none -> 1.43 us  [the longest x1 1.17 us: split_up(): return jnp.moveaxis(value.reshape(*before, size, -1, *after), dim, 0)]
    another operation x0 -> x2, local copies, waits for them, and re-layouts: none -> 0.91 us
    gather x0 -> x2, local copies, waits for them, and re-layouts: none -> 0.88 us  [body(): blocks_2 = jnp.stack(gathered_2)[place ^ jnp.arange(devices)]]
  transfers between devices with their start and end apart: 3 -> 9, of which waited for: 2 -> 4; matrix products, arithmetic and copies ran while one was open for 7% -> 8% of each run, Pallas kernels for 0% -> 0%
where the time goes in v1:
time: 45.5 us; the launch traced here: 45.3 us
  starting transfers between devices  13.9 us (31%)
  waiting for transfers between devices  9.51 us (21%)
  blocking collectives  9.29 us (20%)
  local copies, waits for them, and re-layouts  7.76 us (17%)
  matrix products  3.4 us (7%)
  other arithmetic  1.1 us (2%)
    ppermute x7, starting transfers between devices, body(): lax.ppermute(sent, 'head', [(i, i ^ step) for i in range(devices)])  13.3 us
    all_to_all x1, blocking collectives, body(): lax.all_to_all(output, 'head', split_axis=0, concat_axis=1, tiled=True)  9.29 us
    ppermute x7, waiting for transfers between devices, body(): lax.ppermute(sent, 'head', [(i, i ^ step) for i in range(devices)])  6.25 us
    ppermute x2, waiting for transfers between devices, from_behind(): return lax.ppermute(value, axis, pairs)  3.27 us
    gather x3, local copies, waits for them, and re-layouts, attend(): tiles = source.reshape(blocks, BLOCK, 2 * head_dim)[chosen]  2.1 us
    dot_general x3, matrix products, attend(): jnp.einsum('nqk,nkd->nqd', weights.astype(jnp.bfloat16), value_part, pref...  1.75 us
    dot_general x3, matrix products, attend(): jnp.einsum('nqd,nkd->nqk', query, key_part, preferred_element_type=jnp.fl...  1.64 us
    reshape x1, local copies, waits for them, and re-layouts, split_up(): return jnp.moveaxis(value.reshape(*before, size, -1, *after), dim, 0)  1.17 us
  transfers between devices with their start and end apart: 9, of which 4 were waited for; matrix products, arithmetic and copies ran while one was open for 8% of the time, Pallas kernels for 0%

profile of v1, /device:TPU:0, one launch (start us, length us, event | category | flops | bytes accessed | tf_op | source)
XLA Modules:
  0.0 45.3 jit_solution(12771732293963914813)
XLA Ops:
  0.0 1.2 %reshape.305 = bf16[64,3,8,64]{3,2,0,1:T(8,128)(2,1)S(1)} reshape(bf16[64,3,512]{2,0,1:T(8,128)(2,1)} %param.3) | data formatting | bytes 393216 | tf_op jit(solution)/shard_map/reshape | solution.py:11
  1.2 0.9 %constant_dynamic-slice_fusion = (bf16[64,3,1,64]{3,2,0,1:T(2,128)(2,1)S(1)}, bf16[64,3,1,64]{3,2,0,1:T(2,128)(2,1)S(1)}, bf16[64,3,1,64]{3,2,0,1:T(2,128)(2,1)S...) fusion(bf16[64,3,8,64]{3,2,0,1:T(8,128)(2,1)S(1)} %reshape.305,, ...), kind=kLoop, calls=%fused_computation.73 | loop fusion | bytes 393248 | tf_op jit(solution)/shard_map/dynamic-slice.8
  2.1 3.1 %collective-permute-start = (bf16[64,3,64]{2,0,1:T(8,128)(2,1)S(1)}, bf16[64,3,64]{2,0,1:T(8,128)(2,1)S(1)}, u32[]{:S(2)}, u32[]{:S(2)}) collective-permute-start(bf16[64,3,64]{2,0,1:T(8,128)(2,1)S(1)} %bitcast.97), channel_id=1, source_target_pairs={{0,1},{1,0},{2,3},{3,2},{4,5},{5,4},{6,7},{7,6},{8,9},{9,8},{10,11... | collective-permute-start | bytes 73736 | tf_op jit(solution)/shard_map/ppermute | solution.py:33
  5.2 1.6 %collective-permute-start.1 = (bf16[64,3,64]{2,0,1:T(8,128)(2,1)S(1)}, bf16[64,3,64]{2,0,1:T(8,128)(2,1)S(1)}, u32[]{:S(2)}, u32[]{:S(2)}) collective-permute-start(bf16[64,3,64]{2,0,1:T(8,128)(2,1)S(1)} %bitcast.96), channel_id=1, source_target_pairs={{0,2},{1,3},{2,0},{3,1},{4,6},{5,7},{6,4},{7,5},{8,10},{9,11},{10,... | collective-permute-start | bytes 73736 | tf_op jit(solution)/shard_map/ppermute | solution.py:33
  6.9 0.1 collective-permute-start.2
  7.0 3.0 %collective-permute-start.3 = (bf16[64,3,64]{2,0,1:T(8,128)(2,1)S(1)}, bf16[64,3,64]{2,0,1:T(8,128)(2,1)S(1)}, u32[]{:S(2)}, u32[]{:S(2)}) collective-permute-start(bf16[64,3,64]{2,0,1:T(8,128)(2,1)S(1)} %bitcast.94), channel_id=1, source_target_pairs={{0,4},{1,5},{2,6},{3,7},{4,0},{5,1},{6,2},{7,3},{8,12},{9,13},{10,... | collective-permute-start | bytes 73736 | tf_op jit(solution)/shard_map/ppermute | solution.py:33
  10.0 0.0 copy-start.1
  10.0 0.0 copy-start
  10.0 1.4 %collective-permute-start.4 = (bf16[64,3,64]{2,0,1:T(8,128)(2,1)S(1)}, bf16[64,3,64]{2,0,1:T(8,128)(2,1)S(1)}, u32[]{:S(2)}, u32[]{:S(2)}) collective-permute-start(bf16[64,3,64]{2,0,1:T(8,128)(2,1)S(1)} %bitcast.93), channel_id=1, source_target_pairs={{0,5},{1,4},{2,7},{3,6},{4,1},{5,0},{6,3},{7,2},{8,13},{9,12},{10,... | collective-permute-start | bytes 73736 | tf_op jit(solution)/shard_map/ppermute | solution.py:33
  11.4 0.0 copy-done.1
  11.4 0.0 copy-done
  11.4 0.1 copy.37
  11.5 0.1 reshape.330
  11.6 0.1 copy.33
  11.7 0.1 reshape.322
  11.8 0.1 copy.41
  11.9 0.1 reshape.338
  12.0 0.1 broadcast_compare_fusion.1
  12.1 0.0 collective-permute-done
  12.1 3.7 %collective-permute-start.5 = (bf16[64,3,64]{2,0,1:T(8,128)(2,1)S(1)}, bf16[64,3,64]{2,0,1:T(8,128)(2,1)S(1)}, u32[]{:S(2)}, u32[]{:S(2)}) collective-permute-start(bf16[64,3,64]{2,0,1:T(8,128)(2,1)S(1)} %bitcast.99), channel_id=1, source_target_pairs={{0,6},{1,7},{2,4},{3,5},{4,2},{5,3},{6,0},{7,1},{8,14},{9,15},{10,... | collective-permute-start | bytes 73736 | tf_op jit(solution)/shard_map/ppermute | solution.py:33
  15.8 0.0 collective-permute-done.1
  15.8 0.5 %collective-permute-start.6 = (bf16[64,3,64]{2,0,1:T(8,128)(2,1)S(1)}, bf16[64,3,64]{2,0,1:T(8,128)(2,1)S(1)}, u32[]{:S(2)}, u32[]{:S(2)}) collective-permute-start(bf16[64,3,64]{2,0,1:T(8,128)(2,1)S(1)} %bitcast.98), channel_id=1, source_target_pairs={{0,7},{1,6},{2,5},{3,4},{4,3},{5,2},{6,1},{7,0},{8,15},{9,14},{10,... | collective-permute-start | bytes 73736 | tf_op jit(solution)/shard_map/ppermute | solution.py:33
  16.3 0.0 collective-permute-done.2
  16.4 0.0 collective-permute-done.3
  16.4 0.8 %collective-permute-done.4 = bf16[64,3,64]{2,0,1:T(8,128)(2,1)S(1)} collective-permute-done((bf16[64,3,64]{2,0,1:T(8,128)(2,1)S(1)}, bf16[64,3,64]{2,0,1:T(8,128)(2,1)S(1)}, u32[]{:S(2)}, u32[]{:S(2)}) %collective-permute-start.4) | collective-permute-done | bytes 24608 | tf_op jit(solution)/shard_map/ppermute | solution.py:33
  17.2 0.8 %collective-permute-done.5 = bf16[64,3,64]{2,0,1:T(8,128)(2,1)S(1)} collective-permute-done((bf16[64,3,64]{2,0,1:T(8,128)(2,1)S(1)}, bf16[64,3,64]{2,0,1:T(8,128)(2,1)S(1)}, u32[]{:S(2)}, u32[]{:S(2)}) %collective-permute-start.5) | collective-permute-done | bytes 24608 | tf_op jit(solution)/shard_map/ppermute | solution.py:33
  18.1 4.6 %collective-permute-done.6 = bf16[64,3,64]{2,0,1:T(8,128)(2,1)S(1)} collective-permute-done((bf16[64,3,64]{2,0,1:T(8,128)(2,1)S(1)}, bf16[64,3,64]{2,0,1:T(8,128)(2,1)S(1)}, u32[]{:S(2)}, u32[]{:S(2)}) %collective-permute-start.6) | collective-permute-done | bytes 24608 | tf_op jit(solution)/shard_map/ppermute | solution.py:33
  22.7 0.6 %gather_fusion = bf16[8,64,3,64]{3,1,2,0:T(8,128)(2,1)S(1)} fusion(bf16[8,64,3,64]{3,1,2,0:T(8,128)(2,1)S(1)} %bitcast_dynamic-update-slice_fusion.1, s32[1024]{0:T(1024)S(1)} %pad_clamp_fusion.3), kind=kCustom, calls=%fused_computation | custom fusion | bytes 393248 | tf_op jit(solution)/shard_map/gather | solution.py:34
  23.3 0.3 copy.29
  23.6 0.3 reshape.306
  23.9 0.1 collective-permute-start.8
  23.9 0.5 %collective-permute-start.7 = (bf16[512,128]{0,1:T(8,128)(2,1)S(1)}, bf16[512,128]{0,1:T(8,128)(2,1)S(1)}, u32[]{:S(2)}, u32[]{:S(2)}) collective-permute-start(bf16[512,128]{0,1:T(8,128)(2,1)S(1)} %pad_maximum_fusion.1), channel_id=1, source_target_pairs={{0,8},{8,16},{16,24},{24,0},{1,9},{9,17},{17,25},{25,1},{2,10},{10... | collective-permute-start | bytes 393224 | tf_op jit(solution)/shard_map/while/body/eval_jaxpr/ppermute | solution.py:23
  24.4 0.1 copy.32
  24.6 0.1 copy.31
  24.7 0.1 copy.30
  24.8 0.1 pad_maximum_fusion
  24.9 0.7 %gather_fusion.1 = bf16[48,64,128]{2,1,0:T(8,128)(2,1)S(1)} fusion(bf16[8,64,128]{2,1,0:T(8,128)(2,1)S(1)} %pad_maximum_fusion, s32[1024]{0:T(1024)S(1)} %pad_clamp_fusion.2), kind=kCustom, calls=%fused_computation.1 | custom fusion | bytes 1573056 | tf_op jit(solution)/shard_map/gather | solution.py:49
  25.6 0.5 %fusion.30 = (f32[8,64]{1,0:T(8,128)S(1)}, f32[8,64,384]{2,1,0:T(8,128)S(1)}) fusion(bf16[8,64,64]{2,1,0:T(8,128)(2,1)S(1)} %bitcast.87, bf16[8,384,128]{2,1,0:T(8,128)(2,1)S(1)} %bitcast.79, pred[8,384]{1,0:T(8,128)(4,1)S(1)} %get-tuple-element.59), kind=kOutput, calls=%fused_computation.89 | convolution fusion | flops 25755136 | bytes 1643520 | tf_op jit(solution)/shard_map/nqd,nkd->nqk/dot_general | solution.py:54
  26.2 0.3 fusion.13
  26.5 3.3 %collective-permute-done.7 = bf16[512,128]{0,1:T(8,128)(2,1)S(1)} collective-permute-done((bf16[512,128]{0,1:T(8,128)(2,1)S(1)}, bf16[512,128]{0,1:T(8,128)(2,1)S(1)}, u32[]{:S(2)}, u32[]{:S(2)}) %collective-permute-start.7) | collective-permute-done | bytes 131104 | tf_op jit(solution)/shard_map/while/body/eval_jaxpr/ppermute | solution.py:23
  29.8 0.1 copy.36
  29.9 0.7 %gather_fusion.2 = bf16[48,64,128]{2,1,0:T(8,128)(2,1)S(1)} fusion(bf16[8,64,128]{2,1,0:T(8,128)(2,1)S(1)} %bitcast.83, s32[1024]{0:T(1024)S(1)} %pad_clamp_fusion.1), kind=kCustom, calls=%fused_computation.2 | custom fusion | bytes 1573056 | tf_op jit(solution)/shard_map/while/body/eval_jaxpr/gather | solution.py:49
  30.6 0.0 collective-permute-done.8
  30.6 0.1 copy.40
  30.7 0.7 %gather_fusion.3 = bf16[48,64,128]{2,1,0:T(8,128)(2,1)S(1)} fusion(bf16[8,64,128]{2,1,0:T(8,128)(2,1)S(1)} %bitcast.84, s32[1024]{0:T(1024)S(1)} %pad_clamp_fusion), kind=kCustom, calls=%fused_computation.3 | custom fusion | bytes 1573056 | tf_op jit(solution)/shard_map/while/body/eval_jaxpr/gather | solution.py:49
  31.5 0.5 %fusion.31 = (f32[8,64]{1,0:T(8,128)S(1)}, f32[8,64,384]{2,1,0:T(8,128)S(1)}) fusion(bf16[8,64,64]{2,1,0:T(8,128)(2,1)S(1)} %bitcast.88, bf16[8,384,128]{2,1,0:T(8,128)(2,1)S(1)} %bitcast.85, pred[8,384]{1,0:T(8,128)(4,1)S(1)} %get-tuple-element.58), kind=kOutput, calls=%fused_computation.90 | convolution fusion | flops 25755136 | bytes 1643520 | tf_op jit(solution)/shard_map/while/body/eval_jaxpr/nqd,nkd->nqk/dot_general | solution.py:54
  32.0 0.6 %fusion.32 = (f32[8,64]{1,0:T(8,128)S(1)}, f32[8,64,384]{2,1,0:T(8,128)S(1)}) fusion(bf16[8,64,64]{2,1,0:T(8,128)(2,1)S(1)} %bitcast.89, bf16[8,384,128]{2,1,0:T(8,128)(2,1)S(1)} %bitcast.81, pred[8,384]{1,0:T(8,128)(4,1)S(1)} %get-tuple-element.57), kind=kOutput, calls=%fused_computation.91 | convolution fusion | flops 25755136 | bytes 1643520 | tf_op jit(solution)/shard_map/while/body/eval_jaxpr/nqd,nkd->nqk/dot_general | solution.py:54
  32.6 0.5 %fusion.15 = (f32[8,64]{1,0:T(8,128)S(1)}, f32[8,64]{1,0:T(8,128)S(1)}) fusion(f32[8,64,384]{2,1,0:T(8,128)S(1)} %get-tuple-element.68, f32[8,64]{1,0:T(8,128)S(1)} %get-tuple-element.27, f32[8,64,384]{2,1,0:T(8,128)S(1)} %get-tuple-element.66, f32[8,64]{1,0:T(8,128)S(1)} %get-tuple-element.26), kind=kLoop, calls=%fused_computation.28 | loop fusion | flops 785408 | bytes 1581056 | tf_op jit(solution)/shard_map/while/body/eval_jaxpr/reduce_sum | solution.py:62
  33.1 0.6 %fusion.5 = f32[8,64,64]{2,1,0:T(8,128)S(1)} fusion(bf16[8,384,128]{2,1,0:T(8,128)(2,1)S(1)} %bitcast.80, f32[8,64,384]{2,1,0:T(8,128)S(1)} %get-tuple-element.64, f32[8,64]{1,0:T(8,128)S(1)} %get-tuple-element.63, f32[8,64]{1,0:T(8,128)S(1)} %get-tuple-element.25, f32[8,64]{1,0:T(8,128)S(1)} %get-tuple-element.56), kind=kOutput, calls=%fused_computation.15 | convolution fusion | flops 25624576 | bytes 1710080 | tf_op jit(solution)/shard_map/nqk,nkd->nqd/dot_general | solution.py:63
  33.7 0.6 %fusion.4 = f32[8,64,64]{2,1,0:T(8,128)S(1)} fusion(f32[8,64,64]{2,1,0:T(8,128)S(1)} %fusion.5, bf16[8,384,128]{2,1,0:T(8,128)(2,1)S(1)} %bitcast.82, f32[8,64,384]{2,1,0:T(8,128)S(1)} %get-tuple-element.68, f32[8,64]{1,0:T(8,128)S(1)} %get-tuple-element.27, f32[8,64]{1,0:T(8,128)S(1)} %get-tuple-element.24), kind=kOutput, calls=%fused_computation.13 | convolution fusion | flops 25624576 | bytes 1839104 | tf_op jit(solution)/shard_map/while/body/eval_jaxpr/nqk,nkd->nqd/dot_general | solution.py:63
  34.3 0.6 %fusion.6 = bf16[8,64,64]{2,1,0:T(8,128)(2,1)S(1)} fusion(f32[8,64,64]{2,1,0:T(8,128)S(1)} %fusion.4, bf16[8,384,128]{2,1,0:T(8,128)(2,1)S(1)} %bitcast.86, f32[8,64,384]{2,1,0:T(8,128)S(1)} %get-tuple-element.66, f32[8,64]{1,0:T(8,128)S(1)} %get-tuple-element.26, f32[8,64]{1,0:T(8,128)S(1)} %get-tuple-element.23), kind=kOutput, calls=%fused_computation.16 | convolution fusion | flops 25657344 | bytes 1773568 | tf_op jit(solution)/shard_map/while/body/eval_jaxpr/nqk,nkd->nqd/dot_general | solution.py:63
  34.9 0.2 reshape.350
  35.0 9.3 %all_to_all.16 = bf16[8,2,2048]{2,1,0:T(2,128)(2,1)S(1)} all-to-all(bf16[8,2,2048]{2,1,0:T(2,128)(2,1)S(1)} %reshape.350), channel_id=1, replica_groups=mesh['group'=4,'head'=8] {'head'}, dimensions={0} | all-to-all | bytes 131072 | tf_op jit(solution)/shard_map/all_to_all | solution.py:89
  44.3 0.1 reshape.351
  44.5 0.1 copy.44
  44.6 0.8 %all_to_all.14 = bf16[64,512]{1,0:T(8,128)(2,1)} reshape(bf16[64,8,64]{2,1,0:T(8,128)(2,1)S(1)} %copy.44) | data formatting | bytes 131072 | tf_op jit(solution)/shard_map/all_to_all | solution.py:89
  (27 shorter events, 0.3 us)
Async XLA Ops:
  2.1 10.0 %collective-permute-start = (bf16[64,3,64]{2,0,1:T(8,128)(2,1)S(1)}, bf16[64,3,64]{2,0,1:T(8,128)(2,1)S(1)}, u32[]{:S(2)}, u32[]{:S(2)}) collective-permute-start(bf16[64,3,64]{2,0,1:T(8,128)(2,1)S(1)} %bitcast.97), channel_id=1, source_target_pairs={{0,1},{1,0},{2,3},{3,2},{4,5},{5,4},{6,7},{7,6},{8,9},{9,8},{10,11... | collective-permute-start | bytes 73736 | tf_op jit(solution)/shard_map/ppermute | solution.py:33
  5.2 10.6 %collective-permute-start.1 = (bf16[64,3,64]{2,0,1:T(8,128)(2,1)S(1)}, bf16[64,3,64]{2,0,1:T(8,128)(2,1)S(1)}, u32[]{:S(2)}, u32[]{:S(2)}) collective-permute-start(bf16[64,3,64]{2,0,1:T(8,128)(2,1)S(1)} %bitcast.96), channel_id=1, source_target_pairs={{0,2},{1,3},{2,0},{3,1},{4,6},{5,7},{6,4},{7,5},{8,10},{9,11},{10,... | collective-permute-start | bytes 73736 | tf_op jit(solution)/shard_map/ppermute | solution.py:33
  6.9 9.5 %collective-permute-start.2 = (bf16[64,3,64]{2,0,1:T(8,128)(2,1)S(1)}, bf16[64,3,64]{2,0,1:T(8,128)(2,1)S(1)}, u32[]{:S(2)}, u32[]{:S(2)}) collective-permute-start(bf16[64,3,64]{2,0,1:T(8,128)(2,1)S(1)} %bitcast.95), channel_id=1, source_target_pairs={{0,3},{1,2},{2,1},{3,0},{4,7},{5,6},{6,5},{7,4},{8,11},{9,10},{10,... | collective-permute-start | bytes 73736 | tf_op jit(solution)/shard_map/ppermute | solution.py:33
  7.0 9.4 %collective-permute-start.3 = (bf16[64,3,64]{2,0,1:T(8,128)(2,1)S(1)}, bf16[64,3,64]{2,0,1:T(8,128)(2,1)S(1)}, u32[]{:S(2)}, u32[]{:S(2)}) collective-permute-start(bf16[64,3,64]{2,0,1:T(8,128)(2,1)S(1)} %bitcast.94), channel_id=1, source_target_pairs={{0,4},{1,5},{2,6},{3,7},{4,0},{5,1},{6,2},{7,3},{8,12},{9,13},{10,... | collective-permute-start | bytes 73736 | tf_op jit(solution)/shard_map/ppermute | solution.py:33
  10.0 1.4 %copy-start.1 = (s32[1,3,8]{2,0,1:T(1,128)S(1)}, s32[1,3,8]{2,0,1:T(1,128)}, u32[]{:S(2)}) copy-start(s32[1,3,8]{2,0,1:T(1,128)} %param.5) | copy-start | bytes 292
  10.0 1.4 %copy-start = (s32[1,3,8,6]{2,0,3,1:T(1,128)S(1)}, s32[1,3,8,6]{2,0,3,1:T(1,128)}, u32[]{:S(2)}) copy-start(s32[1,3,8,6]{2,0,3,1:T(1,128)} %param.4) | copy-start | bytes 1732
  10.0 7.2 %collective-permute-start.4 = (bf16[64,3,64]{2,0,1:T(8,128)(2,1)S(1)}, bf16[64,3,64]{2,0,1:T(8,128)(2,1)S(1)}, u32[]{:S(2)}, u32[]{:S(2)}) collective-permute-start(bf16[64,3,64]{2,0,1:T(8,128)(2,1)S(1)} %bitcast.93), channel_id=1, source_target_pairs={{0,5},{1,4},{2,7},{3,6},{4,1},{5,0},{6,3},{7,2},{8,13},{9,12},{10,... | collective-permute-start | bytes 73736 | tf_op jit(solution)/shard_map/ppermute | solution.py:33
  12.1 6.0 %collective-permute-start.5 = (bf16[64,3,64]{2,0,1:T(8,128)(2,1)S(1)}, bf16[64,3,64]{2,0,1:T(8,128)(2,1)S(1)}, u32[]{:S(2)}, u32[]{:S(2)}) collective-permute-start(bf16[64,3,64]{2,0,1:T(8,128)(2,1)S(1)} %bitcast.99), channel_id=1, source_target_pairs={{0,6},{1,7},{2,4},{3,5},{4,2},{5,3},{6,0},{7,1},{8,14},{9,15},{10,... | collective-permute-start | bytes 73736 | tf_op jit(solution)/shard_map/ppermute | solution.py:33
  15.8 6.9 %collective-permute-start.6 = (bf16[64,3,64]{2,0,1:T(8,128)(2,1)S(1)}, bf16[64,3,64]{2,0,1:T(8,128)(2,1)S(1)}, u32[]{:S(2)}, u32[]{:S(2)}) collective-permute-start(bf16[64,3,64]{2,0,1:T(8,128)(2,1)S(1)} %bitcast.98), channel_id=1, source_target_pairs={{0,7},{1,6},{2,5},{3,4},{4,3},{5,2},{6,1},{7,0},{8,15},{9,14},{10,... | collective-permute-start | bytes 73736 | tf_op jit(solution)/shard_map/ppermute | solution.py:33
  23.9 6.7 %collective-permute-start.8 = (bf16[512,128]{0,1:T(8,128)(2,1)S(1)}, bf16[512,128]{0,1:T(8,128)(2,1)S(1)}, u32[]{:S(2)}, u32[]{:S(2)}) collective-permute-start(bf16[512,128]{0,1:T(8,128)(2,1)S(1)} %pad_maximum_fusion.1), channel_id=1, source_target_pairs={{0,24},{8,0},{16,8},{24,16},{1,25},{9,1},{17,9},{25,17},{2,26},{10... | collective-permute-start | bytes 393224 | tf_op jit(solution)/shard_map/while/body/eval_jaxpr/ppermute | solution.py:23
  23.9 5.8 %collective-permute-start.7 = (bf16[512,128]{0,1:T(8,128)(2,1)S(1)}, bf16[512,128]{0,1:T(8,128)(2,1)S(1)}, u32[]{:S(2)}, u32[]{:S(2)}) collective-permute-start(bf16[512,128]{0,1:T(8,128)(2,1)S(1)} %pad_maximum_fusion.1), channel_id=1, source_target_pairs={{0,8},{8,16},{16,24},{24,0},{1,9},{9,17},{17,25},{25,1},{2,10},{10... | collective-permute-start | bytes 393224 | tf_op jit(solution)/shard_map/while/body/eval_jaxpr/ppermute | solution.py:23
